TPU v7x, 32 devices: a whole 2x2x4 slice. The times are simulated.
32 devices in a mesh: fsdp: 16 (over z, y, core), sp: 2 (over x).
Axes of the slice: x: 2, y: 2, z: 4, core: 2. Of those that a mesh axis runs over, the one named last changes fastest.
Arguments:
- latents: bfloat16 [32, 256, 768], P('fsdp', 'sp'), may hold values from -6 to 6
- condition: bfloat16 [32, 768], P('fsdp'), may hold values from -6 to 6
- cotangent: bfloat16 [32, 256, 768], P('fsdp', 'sp'), may hold values from -6 to 6
- w_ada: bfloat16 [768, 4608], P('fsdp'), may hold values from -0.21875 to 0.21875
- b_ada: bfloat16 [4608], P('fsdp'), may hold values from -3 to 3
- w_qkv: bfloat16 [768, 2304], P('fsdp'), may hold values from -0.21875 to 0.21875
- b_query: bfloat16 [768], P('fsdp'), may hold values from -3 to 3
- b_value: bfloat16 [768], P('fsdp'), may hold values from -3 to 3
- w_out: bfloat16 [768, 768], P('fsdp'), may hold values from -0.875 to 0.875
- b_out: bfloat16 [768], P('fsdp'), may hold values from -3 to 3
- w_up: bfloat16 [768, 3072], P('fsdp'), may hold values from -0.21875 to 0.21875
- b_up: bfloat16 [3072], P('fsdp'), may hold values from -3 to 3
- w_down: bfloat16 [3072, 768], P('fsdp'), may hold values from -0.109375 to 0.109375
- b_down: bfloat16 [768], P('fsdp'), may hold values from -3 to 3
Outputs:
- output: bfloat16 [32, 256, 768], P('fsdp', 'sp')
- grad_latents: float32 [32, 256, 768], P('fsdp', 'sp')
- grad_condition: float32 [32, 768], P('fsdp')
- grad_w_ada: float32 [768, 4608], P(('fsdp', 'sp'))
- grad_b_ada: float32 [4608], P(('fsdp', 'sp'))
- grad_w_qkv: float32 [768, 2304], P(('fsdp', 'sp'))
- grad_b_query: float32 [768], P(('fsdp', 'sp'))
- grad_b_value: float32 [768], P(('fsdp', 'sp'))
- grad_w_out: float32 [768, 768], P(('fsdp', 'sp'))
- grad_b_out: float32 [768], P(('fsdp', 'sp'))
- grad_w_up: float32 [768, 3072], P(('fsdp', 'sp'))
- grad_b_up: float32 [3072], P(('fsdp', 'sp'))
- grad_w_down: float32 [3072, 768], P(('fsdp', 'sp'))
- grad_b_down: float32 [768], P(('fsdp', 'sp'))
All inputs are finite; a program needn't handle non-finite values.
Results may differ from a plain program's by a relative error of at most 0.015.
The roundings to bfloat16 on the way count: a program that leaves them out, or rounds other values in their place, can miss the bound.
Values may be sent and summed in bfloat16 or wider, within the bound.
A program may use at most 256 MiB of HBM per device.

v0:
```python
import jax
import jax.numpy as jnp
from jax import lax
from jax.sharding import PartitionSpec as P

D = 768
H = 12
HD = 64
eps = 1e-06


def normalize(values):
    centered = values - jnp.mean(values, axis=-1, keepdims=True)
    inverse = lax.rsqrt(jnp.mean(centered * centered, axis=-1, keepdims=True) + eps)
    return (centered * inverse, inverse)


def norm_back(grad_in, normed, inverse):
    return inverse * (
        grad_in
        - jnp.mean(grad_in, axis=-1, keepdims=True)
        - normed * jnp.mean(grad_in * normed, axis=-1, keepdims=True)
    )


def gelu_tanh(values):
    return jax.nn.gelu(values, approximate=True)


def silu_back(values, grad_out):
    return jax.vjp(jax.nn.silu, values)[1](grad_out)[0]


def gelu_back(values, grad_out):
    return jax.vjp(gelu_tanh, values)[1](grad_out)[0]


LANES = 2048


def reduce_rows(grad):
    return lax.psum_scatter(
        grad.astype(jnp.bfloat16), ("fsdp", "sp"), scatter_dimension=0, tiled=True
    ).astype(jnp.float32)


def body(
    latents,
    condition,
    cotangent,
    w_ada,
    b_ada,
    w_qkv,
    b_query,
    b_value,
    w_out,
    b_out,
    w_up,
    b_up,
    w_down,
    b_down,
):
    f32 = jnp.float32
    bf16 = jnp.bfloat16
    fsdp_count = lax.axis_size("fsdp")
    sp_count = lax.axis_size("sp")
    owners = fsdp_count * sp_count
    fsdp_index = lax.axis_index("fsdp")
    sp_index = lax.axis_index("sp")
    owner_index = fsdp_index * sp_count + sp_index
    pair_latents = latents.shape[0]
    own_latents = pair_latents // sp_count
    latent_total = pair_latents * fsdp_count
    tokens_all = latents.shape[1] * sp_count
    scale_factor = HD ** (-0.5)
    small = [condition.reshape(-1), b_ada, b_query, b_value, b_out, b_up, b_down]
    width = sum((part.size for part in small))
    padded = -(-width // LANES) * LANES
    small.append(jnp.zeros((padded - width,), bf16))
    small_all = lax.all_gather(
        jnp.concatenate(small).reshape(1, padded // 128, 128), "fsdp", axis=0, tiled=True
    ).reshape(fsdp_count, padded)
    pieces = []
    start = 0
    for part in small[:-1]:
        pieces.append(small_all[:, start : start + part.size].reshape(-1))
        start = start + part.size
    cond_all, ada_bias, query_bias, value_bias, out_bias, up_bias, down_bias = pieces
    cond_all = cond_all.reshape(latent_total, D).astype(f32)
    silu_all = jax.nn.silu(cond_all)
    inputs = lax.all_to_all(latents, "sp", split_axis=0, concat_axis=1, tiled=True).astype(f32)
    grad_out = lax.all_to_all(cotangent, "sp", split_axis=0, concat_axis=1, tiled=True).astype(f32)
    ada_rows = w_ada.shape[0]
    silu_mine = lax.dynamic_index_in_dim(
        silu_all.astype(bf16).reshape(fsdp_count, sp_count, own_latents, D), sp_index, 1, False
    )
    silu_mine = lax.dynamic_index_in_dim(
        silu_mine.reshape(fsdp_count * own_latents, fsdp_count, ada_rows), fsdp_index, 1, False
    )
    mod_part = jnp.dot(silu_mine, w_ada, preferred_element_type=f32)
    mod_part = lax.all_to_all(
        mod_part.reshape(fsdp_count, own_latents * 6 * D),
        "fsdp",
        split_axis=0,
        concat_axis=0,
        tiled=True,
    )
    modulate = jnp.sum(mod_part, axis=0).reshape(own_latents, 6 * D) + ada_bias.astype(f32)
    mod_parts = modulate.reshape(own_latents, 6, 1, D)
    shift_one, scale_one, gate_one = (mod_parts[:, 0], mod_parts[:, 1], mod_parts[:, 2])
    shift_two, scale_two, gate_two = (mod_parts[:, 3], mod_parts[:, 4], mod_parts[:, 5])
    qkv_full = lax.all_gather(w_qkv, "fsdp", axis=0, tiled=True)
    out_full = lax.all_gather(w_out, "fsdp", axis=0, tiled=True)
    up_full = lax.all_gather(w_up, "fsdp", axis=0, tiled=True)
    down_full = lax.all_gather(w_down, "fsdp", axis=0, tiled=True)
    normed_one, inverse_one = normalize(inputs)
    attn_in = (normed_one * (1.0 + scale_one) + shift_one).astype(bf16)
    qkv_bias = jnp.concatenate([query_bias, jnp.zeros_like(query_bias), value_bias]).astype(f32)
    projected = (
        jnp.einsum("btd,de->bte", attn_in, qkv_full, preferred_element_type=f32) + qkv_bias
    ).astype(bf16)
    heads = projected.reshape(own_latents, tokens_all, 3, H, HD).transpose(2, 0, 3, 1, 4)
    queries, key_heads, value_heads = (heads[0], heads[1], heads[2])
    scores = (
        jnp.einsum("bhqd,bhkd->bhqk", queries, key_heads, preferred_element_type=f32) * scale_factor
    )
    log_total = jnp.log(jnp.sum(jnp.exp(scores), axis=-1, keepdims=True))
    soft_float = jnp.exp(scores - log_total)
    soft_half = soft_float.astype(bf16)
    mixed = jnp.einsum(
        "bhqk,bhkd->bhqd", soft_half, value_heads, preferred_element_type=f32
    ).astype(bf16)
    mixed_tokens = mixed.transpose(0, 2, 1, 3).reshape(own_latents, tokens_all, D)
    attn_proj = jnp.einsum(
        "btd,de->bte", mixed_tokens, out_full, preferred_element_type=f32
    ) + out_bias.astype(f32)
    residual = inputs + gate_one * attn_proj
    normed_two, inverse_two = normalize(residual)
    mlp_in = (normed_two * (1.0 + scale_two) + shift_two).astype(bf16)
    up_value = jnp.einsum(
        "btd,df->btf", mlp_in, up_full, preferred_element_type=f32
    ) + up_bias.astype(f32)
    activated = gelu_tanh(up_value).astype(bf16)
    down_value = jnp.einsum(
        "btf,fd->btd", activated, down_full, preferred_element_type=f32
    ) + down_bias.astype(f32)
    output = (residual + gate_two * down_value).astype(bf16)
    output = lax.all_to_all(output, "sp", split_axis=1, concat_axis=0, tiled=True)
    grad_gate_two = jnp.sum(grad_out * down_value, axis=1)
    grad_down = (grad_out * gate_two).astype(bf16)
    gw_down = jnp.einsum("btf,btd->fd", activated, grad_down, preferred_element_type=f32)
    own_down = reduce_rows(gw_down)
    gb_down = jnp.sum(grad_down.astype(f32), axis=(0, 1))
    grad_act = jnp.einsum("btd,fd->btf", grad_down, down_full, preferred_element_type=f32)
    grad_up = gelu_back(up_value, grad_act).astype(bf16)
    gw_up = jnp.einsum("btd,btf->df", mlp_in, grad_up, preferred_element_type=f32)
    own_up = reduce_rows(gw_up)
    gb_up = jnp.sum(grad_up.astype(f32), axis=(0, 1))
    grad_mlp = jnp.einsum("btf,df->btd", grad_up, up_full, preferred_element_type=f32)
    grad_scale_two = jnp.sum(grad_mlp * normed_two, axis=1)
    grad_shift_two = jnp.sum(grad_mlp, axis=1)
    grad_resid = grad_out + norm_back(grad_mlp * (1.0 + scale_two), normed_two, inverse_two)
    grad_gate_one = jnp.sum(grad_resid * attn_proj, axis=1)
    grad_proj = (grad_resid * gate_one).astype(bf16)
    gw_out = jnp.einsum("btd,bte->de", mixed_tokens, grad_proj, preferred_element_type=f32)
    own_out = reduce_rows(gw_out)
    gb_out = jnp.sum(grad_proj.astype(f32), axis=(0, 1))
    grad_mixed = jnp.einsum("bte,de->btd", grad_proj, out_full, preferred_element_type=f32).astype(
        bf16
    )
    grad_heads = grad_mixed.reshape(own_latents, tokens_all, H, HD).transpose(0, 2, 1, 3)
    grad_soft = jnp.einsum("bhqd,bhkd->bhqk", grad_heads, value_heads, preferred_element_type=f32)
    delta_sum = jnp.sum(soft_float * grad_soft, axis=-1, keepdims=True)
    grad_scores = (soft_float * (grad_soft - delta_sum)).astype(bf16)
    grad_queries = (
        jnp.einsum("bhqk,bhkd->bhqd", grad_scores, key_heads, preferred_element_type=f32)
        * scale_factor
    ).astype(bf16)
    grad_keys = (
        jnp.einsum("bhqk,bhqd->bhkd", grad_scores, queries, preferred_element_type=f32)
        * scale_factor
    ).astype(bf16)
    grad_values = jnp.einsum(
        "bhqk,bhqd->bhkd", soft_half, grad_heads, preferred_element_type=f32
    ).astype(bf16)
    grad_tokens = (
        jnp.stack([grad_queries, grad_keys, grad_values], axis=0)
        .transpose(1, 3, 0, 2, 4)
        .reshape(own_latents, tokens_all, 3 * D)
    )
    gw_qkv = jnp.einsum("btd,bte->de", attn_in, grad_tokens, preferred_element_type=f32)
    own_qkv = reduce_rows(gw_qkv)
    grad_tok_float = grad_tokens.astype(f32)
    gb_query = jnp.sum(grad_tok_float[:, :, :D], axis=(0, 1))
    gb_value = jnp.sum(grad_tok_float[:, :, 2 * D :], axis=(0, 1))
    grad_attn_in = jnp.einsum("bte,de->btd", grad_tokens, qkv_full, preferred_element_type=f32)
    grad_scale_one = jnp.sum(grad_attn_in * normed_one, axis=1)
    grad_shift_one = jnp.sum(grad_attn_in, axis=1)
    grad_latents = grad_resid + norm_back(grad_attn_in * (1.0 + scale_one), normed_one, inverse_one)
    grad_latents = lax.all_to_all(grad_latents, "sp", split_axis=1, concat_axis=0, tiled=True)
    grad_small = [
        grad_shift_one.reshape(-1),
        grad_scale_one.reshape(-1),
        grad_gate_one.reshape(-1),
        grad_shift_two.reshape(-1),
        grad_scale_two.reshape(-1),
        grad_gate_two.reshape(-1),
        gb_query,
        gb_value,
        gb_out,
        gb_up,
        gb_down,
    ]
    grad_small_all = lax.all_gather(jnp.concatenate(grad_small), ("fsdp", "sp"), axis=0)
    mod_width = 6 * own_latents * D
    grad_mod = (
        grad_small_all[:, :mod_width]
        .reshape(owners, 6, own_latents, D)
        .transpose(0, 2, 1, 3)
        .reshape(latent_total, 6 * D)
    )
    bias_sums = jnp.sum(grad_small_all[:, mod_width:], axis=0)
    own_bias = []
    start = 0
    for part in grad_small[6:]:
        piece = bias_sums[start : start + part.size].reshape(owners, -1)
        own_bias.append(lax.dynamic_index_in_dim(piece, owner_index, 0, False))
        start = start + part.size
    own_gb_query, own_gb_value, own_gb_out, own_gb_up, own_gb_down = own_bias
    silu_rows = lax.dynamic_index_in_dim(
        silu_all.reshape(latent_total, owners, D // owners), owner_index, 1, False
    )
    own_ada = jnp.dot(silu_rows.T, grad_mod, precision=lax.Precision.HIGHEST)
    own_gb_ada = lax.dynamic_index_in_dim(
        jnp.sum(grad_mod, axis=0).reshape(owners, -1), owner_index, 0, False
    )
    grad_silu = jnp.dot(grad_mod.astype(bf16), w_ada.T, preferred_element_type=f32)
    grad_silu = lax.all_to_all(
        grad_silu.reshape(fsdp_count, pair_latents * ada_rows),
        "fsdp",
        split_axis=0,
        concat_axis=0,
        tiled=True,
    )
    grad_silu = (
        grad_silu.reshape(fsdp_count, pair_latents, ada_rows)
        .transpose(1, 0, 2)
        .reshape(pair_latents, D)
    )
    grad_condition = silu_back(condition.astype(f32), grad_silu)
    return (
        output,
        grad_latents,
        grad_condition,
        own_ada,
        own_gb_ada,
        own_qkv,
        own_gb_query,
        own_gb_value,
        own_out,
        own_gb_out,
        own_up,
        own_gb_up,
        own_down,
        own_gb_down,
    )


def solution(mesh):
    in_specs = (
        P("fsdp", "sp", None),
        P("fsdp", None),
        P("fsdp", "sp", None),
        P("fsdp", None),
        P("fsdp"),
        P("fsdp", None),
        P("fsdp"),
        P("fsdp"),
        P("fsdp", None),
        P("fsdp"),
        P("fsdp", None),
        P("fsdp"),
        P("fsdp", None),
        P("fsdp"),
    )
    out_specs = (
        P("fsdp", "sp", None),
        P("fsdp", "sp", None),
        P("fsdp", None),
        P(("fsdp", "sp"), None),
        P(("fsdp", "sp")),
        P(("fsdp", "sp"), None),
        P(("fsdp", "sp")),
        P(("fsdp", "sp")),
        P(("fsdp", "sp"), None),
        P(("fsdp", "sp")),
        P(("fsdp", "sp"), None),
        P(("fsdp", "sp")),
        P(("fsdp", "sp"), None),
        P(("fsdp", "sp")),
    )
    return jax.shard_map(body, mesh=mesh, in_specs=in_specs, out_specs=out_specs, check_vma=False)
```

profile of v0, /device:TPU:0, one launch (start us, length us, event | category | flops | bytes accessed | tf_op | source)
XLA Modules:
  0.0 743.5 jit_solution(2040132775007080298)
XLA Ops:
  8.0 0.7 all-gather.10.cloned.1.call-update
  10.0 4.2 all-to-all-start
  14.2 0.7 reshape.743
  14.9 4.1 concatenate.17
  19.1 22.7 %all_gather.21 = bf16[16,32,128]{2,1,0:T(8,128)(2,1)S(1)} all-gather(bf16[1,32,128]{2,1,0:T(8,128)(2,1)S(1)} %bitcast.185), channel_id=1, replica_groups=mesh['fsdp'=16,'sp'=2] {'fsdp'}, dimensions={0}, use_global_device_ids=true | all-gather | bytes 139264 | tf_op jit(solution)/shard_map/all_gather | solution.py:80
  42.4 1.0 copy.61
  43.7 3.5 all-to-all-start.1
  48.0 13.6 %all-to-all-done.1 = f32[16,1,4608]{2,1,0:T(1,128)S(1)} async-done(((f32[16,1,4608]{2,1,0:T(1,128)}), f32[16,1,4608]{2,1,0:T(1,128)S(1)}, u32[]{:S(2)}, u32[]{:S(2)}) %all-to-all-start.1) | async-done | bytes 294944 | tf_op jit(solution)/shard_map/all_to_all | solution.py:101
  61.7 3.8 all-to-all-start.3
  65.8 6.4 all-to-all-done.3
  72.3 0.8 fusion.21
  73.4 4.2 fusion.1
  77.6 1.6 copy.62
  79.1 2.3 fusion.55
  81.4 4.8 convolution_convert_fusion.4
  86.2 18.5 %all-gather.10.cloned.1.call-done = bf16[768,768]{1,0:T(8,128)(2,1)} async-done(((bf16[48,768]{1,0:T(8,128)(2,1)}), bf16[768,768]{1,0:T(8,128)(2,1)}) %all-gather.10.cloned.1.call-update) | async-done | bytes 1179664 | tf_op jit(solution)/shard_map/all_gather | solution.py:113
  104.6 2.8 fusion.81
  107.7 51.3 %all-gather.14.cloned.1.call-done = bf16[3072,768]{1,0:T(8,128)(2,1)} async-done(((bf16[192,768]{1,0:T(8,128)(2,1)}), bf16[3072,768]{1,0:T(8,128)(2,1)}) %all-gather.14.cloned.1.call-update) | async-done | bytes 4718608 | tf_op jit(solution)/shard_map/all_gather | solution.py:115
  159.0 5.5 fusion.83
  164.5 48.3 %all-gather.12.cloned.1.call-done = bf16[768,3072]{1,0:T(8,128)(2,1)} async-done(((bf16[48,3072]{1,0:T(8,128)(2,1)}), bf16[768,3072]{1,0:T(8,128)(2,1)}) %all-gather.12.cloned.1.call-update) | async-done | bytes 4718608 | tf_op jit(solution)/shard_map/all_gather | solution.py:114
  212.8 7.0 convert_reduce_fusion
  219.9 1.8 multiply_reduce_fusion.1
  222.2 1.7 copy-done.3
  223.9 3.2 fusion.22
  227.1 0.7 copy-done.10
  228.4 0.9 copy.66
  229.3 4.8 fusion.17
  234.7 1.3 copy-done.1
  236.0 2.9 multiply_reduce_fusion
  239.5 1.3 fusion.19
  240.8 1.2 fusion.18
  242.0 1.5 convolution_convert_fusion.3
  243.5 1.4 pad_maximum_fusion
  244.9 4.2 fusion.36
  249.0 1.6 convert.10
  250.7 3.0 multiply_reduce_fusion.2
  255.1 2.9 convolution_convert_fusion.2
  258.1 1.3 copy-done.8
  259.5 3.7 convolution_convert_fusion.1
  264.1 6.3 convolution_convert_fusion
  270.5 1.0 copy-done.13
  272.6 3.0 reduce.57
  275.6 0.8 reshape.788
  276.5 3.5 all-to-all-start.2
  279.9 1.7 copy.70
  281.6 5.5 all-to-all-done.2
  287.2 3.5 all-to-all-start.4
  291.6 0.8 copy.78
  292.4 11.1 %all-to-all-done.4 = f32[1,256,768]{2,0,1:T(1,128)S(1)} async-done(((f32[1,256,768]{2,0,1:T(1,128)}), f32[1,256,768]{2,0,1:T(1,128)S(1)}, u32[]{:S(2)}, u32[]{:S(2)}) %all-to-all-start.4) | async-done | bytes 786464 | tf_op jit(solution)/shard_map/all_to_all | solution.py:200
  303.4 0.9 copy.79
  304.4 42.0 %reduce-scatter.7.cloned.1.call-done = bf16[24,768]{1,0:T(8,128)(2,1)} async-done(((bf16[768,768]{1,0:T(8,128)(2,1)}), bf16[24,768]{1,0:T(8,128)(2,1)}) %reduce-scatter.7.cloned.1.call-update) | async-done | bytes 36880 | tf_op jit(solution)/shard_map/reduce_scatter | solution.py:42
  346.3 1.4 convert_element_type.318
  347.7 55.6 %all-gather.16.cloned.1.call-done = f32[32,1,10752]{2,1,0:T(1,128)} async-done(((f32[1,1,10752]{2,1,0:T(1,128)}), f32[32,1,10752]{2,1,0:T(1,128)}) %all-gather.16.cloned.1.call-update) | async-done | bytes 1376272 | tf_op jit(solution)/shard_map/all_gather | solution.py:214
  403.3 1.4 copy.91
  405.0 0.7 all_to_all.52
  405.7 4.6 all-to-all-start.5
  413.6 1.3 fusion.43
  415.4 1.2 all-to-all-done.5
  418.6 92.5 %reduce-scatter.5.cloned.1.call-done = bf16[24,2304]{1,0:T(8,128)(2,1)} async-done(((bf16[768,2304]{1,0:T(8,128)(2,1)}), bf16[24,2304]{1,0:T(8,128)(2,1)}) %reduce-scatter.5.cloned.1.call-update) | async-done | bytes 110608 | tf_op jit(solution)/shard_map/reduce_scatter | solution.py:42
  511.1 1.6 convert_element_type.316
  512.7 110.3 %reduce-scatter.9.cloned.1.call-done = bf16[24,3072]{1,0:T(8,128)(2,1)} async-done(((bf16[768,3072]{1,0:T(8,128)(2,1)}), bf16[24,3072]{1,0:T(8,128)(2,1)}) %reduce-scatter.9.cloned.1.call-update) | async-done | bytes 147472 | tf_op jit(solution)/shard_map/reduce_scatter | solution.py:42
  623.0 1.6 convert_element_type.320
  624.6 110.7 %reduce-scatter.11.cloned.1.call-done = bf16[96,768]{1,0:T(8,128)(2,1)} async-done(((bf16[3072,768]{1,0:T(8,128)(2,1)}), bf16[96,768]{1,0:T(8,128)(2,1)}) %reduce-scatter.11.cloned.1.call-update) | async-done | bytes 147472 | tf_op jit(solution)/shard_map/reduce_scatter | solution.py:42
  735.3 1.6 convert_element_type.322
  (131 shorter events, 17.1 us)
Async XLA Ops:
  7.2 35.0 %copy-start = (bf16[48,4608]{1,0:T(8,128)(2,1)S(1)}, bf16[48,4608]{1,0:T(8,128)(2,1)}, u32[]{:S(2)}) copy-start(bf16[48,4608]{1,0:T(8,128)(2,1)} %param.17) | copy-start | bytes 1327108
  7.2 66.2 %all-gather.8.cloned.1.call-start = ((), (), s32[]{:S(2)}) async-start(), calls=%async_computation.10 | async-start | bytes 3760128 | tf_op jit(solution)/shard_map/all_gather | solution.py:112
  7.9 96.7 %all-gather.10.cloned.1.call-start = ((), (), s32[]{:S(2)}) async-start(), calls=%async_computation.11 | async-start | bytes 1253376 | tf_op jit(solution)/shard_map/all_gather | solution.py:113
  8.7 150.3 %all-gather.14.cloned.1.call-start = ((), (), s32[]{:S(2)}) async-start(), calls=%async_computation.13 | async-start | bytes 5013504 | tf_op jit(solution)/shard_map/all_gather | solution.py:115
  9.4 203.4 %all-gather.12.cloned.1.call-start = ((), (), s32[]{:S(2)}) async-start(), calls=%async_computation.12 | async-start | bytes 5013504 | tf_op jit(solution)/shard_map/all_gather | solution.py:114
  10.0 33.7 %all-to-all-start = ((bf16[2,128,768]{2,1,0:T(8,128)(2,1)}), bf16[2,128,768]{2,1,0:T(8,128)(2,1)S(1)}, u32[]{:S(2)}, u32[]{:S(2)}) async-start(bf16[2,128,768]{2,1,0:T(8,128)(2,1)} %param.14), calls=%async_computation | async-start | bytes 786432 | tf_op jit(solution)/shard_map/all_to_all | solution.py:91
  43.7 17.9 %all-to-all-start.1 = ((f32[16,1,4608]{2,1,0:T(1,128)}), f32[16,1,4608]{2,1,0:T(1,128)S(1)}, u32[]{:S(2)}, u32[]{:S(2)}) async-start(f32[16,1,4608]{2,1,0:T(1,128)} %copy.61), calls=%async_computation.1 | async-start | bytes 589824 | tf_op jit(solution)/shard_map/all_to_all | solution.py:101
  61.7 10.5 %all-to-all-start.3 = ((bf16[2,128,768]{2,1,0:T(8,128)(2,1)}), bf16[2,128,768]{2,1,0:T(8,128)(2,1)S(1)}, u32[]{:S(2)}, u32[]{:S(2)}) async-start(bf16[2,128,768]{2,1,0:T(8,128)(2,1)} %param.16), calls=%async_computation.3 | async-start | bytes 786432 | tf_op jit(solution)/shard_map/all_to_all | solution.py:92
  65.5 280.9 %reduce-scatter.7.cloned.1.call-start = ((), (), s32[]{:S(2)}) async-start(), calls=%async_computation.15 | async-start | bytes 1216512 | tf_op jit(solution)/shard_map/reduce_scatter | solution.py:42
  212.8 7.1 copy-start.15
  219.8 1.8 copy-start.7
  219.8 2.4 copy-start.16
  219.9 4.0 copy-start.3
  223.9 3.9 copy-start.4
  227.1 0.7 copy-start.10
  229.3 4.8 copy-start.12
  234.1 1.9 copy-start.1
  239.5 2.5 copy-start.9
  239.5 2.5 copy-start.11
  250.7 152.7 %all-gather.16.cloned.1.call-start = ((), (), s32[]{:S(2)}) async-start(), calls=%async_computation.18 | async-start | bytes 1419264 | tf_op jit(solution)/shard_map/all_gather | solution.py:214
  250.7 3.1 copy-start.2
  254.8 256.3 %reduce-scatter.5.cloned.1.call-start = ((), (), s32[]{:S(2)}) async-start(), calls=%async_computation.14 | async-start | bytes 3649536 | tf_op jit(solution)/shard_map/reduce_scatter | solution.py:42
  258.0 1.4 copy-start.8
  258.1 364.9 %reduce-scatter.9.cloned.1.call-start = ((), (), s32[]{:S(2)}) async-start(), calls=%async_computation.16 | async-start | bytes 4866048 | tf_op jit(solution)/shard_map/reduce_scatter | solution.py:42
  263.2 1.0 copy-start.6
  263.2 472.2 %reduce-scatter.11.cloned.1.call-start = ((), (), s32[]{:S(2)}) async-start(), calls=%async_computation.17 | async-start | bytes 4866048 | tf_op jit(solution)/shard_map/reduce_scatter | solution.py:42
  270.5 1.0 copy-start.13
  270.5 9.4 %copy-start.5 = (f32[256,768]{1,0:T(8,128)S(1)}, f32[256,768]{1,0:T(8,128)}, u32[]{:S(2)}) copy-start(f32[256,768]{1,0:T(8,128)} %get-tuple-element.43) | copy-start | bytes 2359300
  276.5 10.7 %all-to-all-start.2 = ((bf16[2,2,49152]{2,1,0:T(2,128)(2,1)}), bf16[2,2,49152]{2,1,0:T(2,128)(2,1)S(1)}, u32[]{:S(2)}, u32[]{:S(2)}) async-start(bf16[2,2,49152]{2,1,0:T(2,128)(2,1)} %reshape.788), calls=%async_computation.2 | async-start | bytes 786432 | tf_op jit(solution)/shard_map/all_to_all | solution.py:148
  287.2 16.3 %all-to-all-start.4 = ((f32[1,256,768]{2,0,1:T(1,128)}), f32[1,256,768]{2,0,1:T(1,128)S(1)}, u32[]{:S(2)}, u32[]{:S(2)}) async-start(f32[1,256,768]{2,0,1:T(1,128)} %copy.70), calls=%async_computation.4 | async-start | bytes 1572864 | tf_op jit(solution)/shard_map/all_to_all | solution.py:200
  347.7 70.2 %copy-start.14 = (bf16[2,768]{1,0:T(2,128)(2,1)S(1)}, bf16[2,768]{1,0:T(2,128)(2,1)}, u32[]{:S(2)}) copy-start(bf16[2,768]{1,0:T(2,128)(2,1)} %param.15) | copy-start | bytes 9220
  405.7 11.0 %all-to-all-start.5 = ((f32[16,1,96]{2,1,0:T(1,128)}), f32[16,1,96]{2,1,0:T(1,128)S(1)}, u32[]{:S(2)}, u32[]{:S(2)}) async-start(f32[16,1,96]{2,1,0:T(1,128)} %bitcast.31), calls=%async_computation.5 | async-start | bytes 16384 | tf_op jit(solution)/shard_map/all_to_all | solution.py:238
Sparse Core Ops, SparseCore 0:
  10.3 55.0 all-gather.7
  67.7 36.8 all-gather.9
  106.9 51.9 all-gather.13
  161.1 51.6 all-gather.11
  250.8 95.5 reduce-scatter.6
  349.6 53.6 all-gather.15
  408.7 102.3 reduce-scatter.4
  516.6 106.3 reduce-scatter.8
  628.5 106.8 reduce-scatter.10
where the time goes:
time: 745 us; the launch traced here: 744 us
  waiting for transfers between devices  570 us (77%)
  matrix products  60.4 us (8%)
  local copies, waits for them, and re-layouts  29.6 us (4%)
  starting transfers between devices  23.8 us (3%)
  other arithmetic  23 us (3%)
  blocking collectives  22.7 us (3%)
  between operations  14.4 us (2%)
    reduce_scatter x4, waiting for transfers between devices, reduce_rows(): lax.psum_scatter(grad.astype(jnp.bfloat16), ('fsdp', 'sp'), scatter_dimen...  355 us
    all_gather x1, waiting for transfers between devices, body(): lax.all_gather(jnp.concatenate(grad_small), ('fsdp', 'sp'), axis=0)  55.6 us
    all_gather x1, waiting for transfers between devices, body(): down_full = lax.all_gather(w_down, 'fsdp', axis=0, tiled=True)  51.3 us
    all_gather x1, waiting for transfers between devices, body(): up_full = lax.all_gather(w_up, 'fsdp', axis=0, tiled=True)  48.3 us
    all_gather x1, blocking collectives, body(): lax.all_gather(jnp.concatenate(small).reshape(1, padded // 128, 128), 'fs...  22.7 us
    all_gather x1, waiting for transfers between devices, body(): out_full = lax.all_gather(w_out, 'fsdp', axis=0, tiled=True)  18.5 us
  transfers between devices with their start and end apart: 15, of which 13 were waited for; matrix products, arithmetic and copies ran while one was open for 9% of the time, Pallas kernels for 0%

commit v1 on v0

--- a/solution.py
+++ b/solution.py
@@ -7,6 +7,27 @@
 H = 12
 HD = 64
 eps = 1e-06
+
+
+def ring_gather(x, axis, dim):
+    length, position, extent = (lax.axis_size(axis), lax.axis_index(axis), x.shape[dim])
+    ahead = [(i, (i + 1) % length) for i in range(length)]
+    left = [(i, (i - 1) % length) for i in range(length)]
+    out = jnp.zeros((*x.shape[:dim], length * extent, *x.shape[dim + 1 :]), x.dtype)
+    out = lax.dynamic_update_slice_in_dim(out, x, position * extent, axis=dim)
+    from_left = from_right = x
+    halfway = length // 2
+    for step in range(1, halfway + 1):
+        from_left = lax.ppermute(from_left, axis, ahead)
+        out = lax.dynamic_update_slice_in_dim(
+            out, from_left, (position - step) % length * extent, axis=dim
+        )
+        if step < length - halfway:
+            from_right = lax.ppermute(from_right, axis, left)
+            out = lax.dynamic_update_slice_in_dim(
+                out, from_right, (position + step) % length * extent, axis=dim
+            )
+    return out
 
 
 def normalize(values):
@@ -112,7 +133,7 @@
     qkv_full = lax.all_gather(w_qkv, "fsdp", axis=0, tiled=True)
     out_full = lax.all_gather(w_out, "fsdp", axis=0, tiled=True)
     up_full = lax.all_gather(w_up, "fsdp", axis=0, tiled=True)
-    down_full = lax.all_gather(w_down, "fsdp", axis=0, tiled=True)
+    down_full = ring_gather(w_down, "fsdp", 0)
     normed_one, inverse_one = normalize(inputs)
     attn_in = (normed_one * (1.0 + scale_one) + shift_one).astype(bf16)
     qkv_bias = jnp.concatenate([query_bias, jnp.zeros_like(query_bias), value_bias]).astype(f32)

time: 745 us -> 700 us (0.940)
  waiting for transfers between devices: 570 us -> 481 us
  starting transfers between devices: 23.8 us -> 56.4 us
  local copies, waits for them, and re-layouts: 29.6 us -> 42.9 us
    all_gather x1 -> x0, waiting for transfers between devices: 51.3 us -> none  [body(): down_full = lax.all_gather(w_down, 'fsdp', axis=0, tiled=True)]
    ppermute x0 -> x15, starting transfers between devices: none -> 33.8 us  [the longest x7 32.8 us: ring_gather(): from_right = lax.ppermute(from_right, axis, left)]
    all_gather x1, waiting for transfers between devices: 48.3 us -> 15.4 us  [body(): up_full = lax.all_gather(w_up, 'fsdp', axis=0, tiled=True)]
    ppermute x0 -> x15, waiting for transfers between devices: none -> 29 us  [the longest x8 24.8 us: ring_gather(): from_left = lax.ppermute(from_left, axis, ahead)]
    all_gather x1, waiting for transfers between devices: 18.5 us -> 0.01 us  [body(): out_full = lax.all_gather(w_out, 'fsdp', axis=0, tiled=True)]
    dynamic_update_slice x0 -> x16, local copies, waits for them, and re-layouts: none -> 12.8 us  [the longest x8 6.97 us: ring_gather(): lax.dynamic_update_slice_in_dim(out, from_left, (position - step) % lengt...]
    all_to_all x1, waiting for transfers between devices: 13.6 us -> 5.92 us  [body(): lax.all_to_all(mod_part.reshape(fsdp_count, own_latents * 6 * D), 'fsdp',...]
  transfers between devices with their start and end apart: 15 -> 29, of which waited for: 13 -> 18; matrix products, arithmetic and copies ran while one was open for 9% -> 11% of each run, Pallas kernels for 0% -> 0%
where the time goes in v1:
time: 700 us; the launch traced here: 699 us
  waiting for transfers between devices  481 us (69%)
  matrix products  60.4 us (9%)
  starting transfers between devices  56.4 us (8%)
  local copies, waits for them, and re-layouts  42.9 us (6%)
  other arithmetic  23 us (3%)
  blocking collectives  19.9 us (3%)
  between operations  15.1 us (2%)
    reduce_scatter x4, waiting for transfers between devices, reduce_rows(): lax.psum_scatter(grad.astype(jnp.bfloat16), ('fsdp', 'sp'), scatter_dimen...  355 us
    all_gather x1, waiting for transfers between devices, body(): lax.all_gather(jnp.concatenate(grad_small), ('fsdp', 'sp'), axis=0)  55.5 us
    ppermute x7, starting transfers between devices, ring_gather(): from_right = lax.ppermute(from_right, axis, left)  32.8 us
    ppermute x8, waiting for transfers between devices, ring_gather(): from_left = lax.ppermute(from_left, axis, ahead)  24.8 us
    all_gather x1, blocking collectives, body(): lax.all_gather(jnp.concatenate(small).reshape(1, padded // 128, 128), 'fs...  19.9 us
    all_gather x1, waiting for transfers between devices, body(): up_full = lax.all_gather(w_up, 'fsdp', axis=0, tiled=True)  15.4 us
  transfers between devices with their start and end apart: 29, of which 18 were waited for; matrix products, arithmetic and copies ran while one was open for 11% of the time, Pallas kernels for 0%

profile of v1, /device:TPU:0, one launch (start us, length us, event | category | flops | bytes accessed | tf_op | source)
XLA Modules:
  0.0 699.0 jit_solution(17748478819968856416)
XLA Ops:
  10.0 5.0 collective-permute-start.1
  15.0 3.5 all-to-all-start
  19.5 4.1 concatenate.17
  23.6 19.9 %all_gather.18 = bf16[16,32,128]{2,1,0:T(8,128)(2,1)S(1)} all-gather(bf16[1,32,128]{2,1,0:T(8,128)(2,1)S(1)} %bitcast.185), channel_id=1, replica_groups=mesh['fsdp'=16,'sp'=2] {'fsdp'}, dimensions={0}, use_global_device_ids=true | all-gather | bytes 139264 | tf_op jit(solution)/shard_map/all_gather | solution.py:101
  45.8 2.5 broadcast_in_dim.8
  49.0 3.5 all-to-all-start.1
  53.3 4.2 collective-permute-start.3
  59.0 5.9 all-to-all-done.1
  64.9 3.5 all-to-all-start.3
  68.8 5.6 collective-permute-start.5
  74.7 4.5 collective-permute-done.4
  80.1 4.4 collective-permute-start.7
  84.6 3.9 collective-permute-done.6
  90.0 4.5 collective-permute-start.9
  95.3 4.5 collective-permute-done.8
  100.5 1.7 constant_dynamic-update-slice_fusion.8
  102.3 4.4 collective-permute-start.11
  107.4 1.7 collective-permute-done.10
  110.9 4.7 collective-permute-start.13
  116.3 1.7 collective-permute-done.12
  119.6 3.9 collective-permute-done.13
  124.2 8.3 %collective-permute-done.14 = bf16[192,768]{1,0:T(8,128)(2,1)S(1)} collective-permute-done((bf16[192,768]{1,0:T(8,128)(2,1)S(1)}, bf16[192,768]{1,0:T(8,128)(2,1)S(1)}, u32[]{:S(2)}, u32[]{:S(2)}) %collective-permute-start.14) | collective-permute-done | bytes 294944 | tf_op jit(solution)/shard_map/ppermute | solution.py:21
  133.3 4.1 fusion.1
  137.4 1.7 copy.62
  139.1 2.3 fusion.55
  141.5 4.8 convolution_convert_fusion.4
  146.2 2.8 fusion.81
  149.3 15.4 %all-gather.11.cloned.1.call-done = bf16[768,3072]{1,0:T(8,128)(2,1)} async-done(((bf16[48,3072]{1,0:T(8,128)(2,1)}), bf16[768,3072]{1,0:T(8,128)(2,1)}) %all-gather.11.cloned.1.call-update) | async-done | bytes 4718608 | tf_op jit(solution)/shard_map/all_gather | solution.py:135
  164.7 4.0 convolution_add_fusion.1
  168.7 6.4 convert_reduce_fusion
  175.1 1.7 multiply_reduce_fusion.1
  176.8 5.6 fusion.22
  184.6 4.8 fusion.17
  190.1 1.3 copy-done.1
  191.4 2.9 multiply_reduce_fusion
  194.9 1.4 fusion.19
  197.4 1.5 convolution_convert_fusion.3
  198.9 1.4 pad_maximum_fusion
  200.3 4.2 fusion.36
  204.5 1.6 convert.10
  206.2 3.0 multiply_reduce_fusion.2
  210.5 2.9 convolution_convert_fusion.2
  213.5 1.3 copy-done.6
  214.9 3.7 convolution_convert_fusion.1
  219.5 6.3 convolution_convert_fusion
  228.0 3.0 reduce.57
  231.9 3.5 all-to-all-start.2
  235.3 1.7 copy.70
  237.0 5.5 all-to-all-done.2
  242.6 3.5 all-to-all-start.4
  247.7 11.1 %all-to-all-done.4 = f32[1,256,768]{2,0,1:T(1,128)S(1)} async-done(((f32[1,256,768]{2,0,1:T(1,128)}), f32[1,256,768]{2,0,1:T(1,128)S(1)}, u32[]{:S(2)}, u32[]{:S(2)}) %all-to-all-start.4) | async-done | bytes 786464 | tf_op jit(solution)/shard_map/all_to_all | solution.py:221
  259.8 42.1 %reduce-scatter.7.cloned.1.call-done = bf16[24,768]{1,0:T(8,128)(2,1)} async-done(((bf16[768,768]{1,0:T(8,128)(2,1)}), bf16[24,768]{1,0:T(8,128)(2,1)}) %reduce-scatter.7.cloned.1.call-update) | async-done | bytes 36880 | tf_op jit(solution)/shard_map/reduce_scatter | solution.py:63
  301.8 1.4 convert_element_type.318
  303.2 55.5 %all-gather.13.cloned.1.call-done = f32[32,1,10752]{2,1,0:T(1,128)} async-done(((f32[1,1,10752]{2,1,0:T(1,128)}), f32[32,1,10752]{2,1,0:T(1,128)}) %all-gather.13.cloned.1.call-update) | async-done | bytes 1376272 | tf_op jit(solution)/shard_map/all_gather | solution.py:235
  358.8 1.4 copy.91
  361.1 4.6 all-to-all-start.5
  369.0 1.3 fusion.43
  370.9 1.2 all-to-all-done.5
  374.1 92.3 %reduce-scatter.5.cloned.1.call-done = bf16[24,2304]{1,0:T(8,128)(2,1)} async-done(((bf16[768,2304]{1,0:T(8,128)(2,1)}), bf16[24,2304]{1,0:T(8,128)(2,1)}) %reduce-scatter.5.cloned.1.call-update) | async-done | bytes 110608 | tf_op jit(solution)/shard_map/reduce_scatter | solution.py:63
  466.4 1.6 convert_element_type.316
  468.0 110.5 %reduce-scatter.9.cloned.1.call-done = bf16[24,3072]{1,0:T(8,128)(2,1)} async-done(((bf16[768,3072]{1,0:T(8,128)(2,1)}), bf16[24,3072]{1,0:T(8,128)(2,1)}) %reduce-scatter.9.cloned.1.call-update) | async-done | bytes 147472 | tf_op jit(solution)/shard_map/reduce_scatter | solution.py:63
  578.5 1.6 convert_element_type.320
  580.1 110.3 %reduce-scatter.11.cloned.1.call-done = bf16[96,768]{1,0:T(8,128)(2,1)} async-done(((bf16[3072,768]{1,0:T(8,128)(2,1)}), bf16[96,768]{1,0:T(8,128)(2,1)}) %reduce-scatter.11.cloned.1.call-update) | async-done | bytes 147472 | tf_op jit(solution)/shard_map/reduce_scatter | solution.py:63
  690.5 1.6 convert_element_type.322
  (180 shorter events, 38.7 us)
Async XLA Ops:
  7.2 36.7 %copy-start = (bf16[48,4608]{1,0:T(8,128)(2,1)S(1)}, bf16[48,4608]{1,0:T(8,128)(2,1)}, u32[]{:S(2)}) copy-start(bf16[48,4608]{1,0:T(8,128)(2,1)} %param.17) | copy-start | bytes 1327108
  7.2 126.1 %all-gather.7.cloned.1.call-start = ((), (), s32[]{:S(2)}) async-start(), calls=%async_computation.10 | async-start | bytes 3760128 | tf_op jit(solution)/shard_map/all_gather | solution.py:133
  7.9 138.3 %all-gather.9.cloned.1.call-start = ((), (), s32[]{:S(2)}) async-start(), calls=%async_computation.11 | async-start | bytes 1253376 | tf_op jit(solution)/shard_map/all_gather | solution.py:134
  8.7 156.0 %all-gather.11.cloned.1.call-start = ((), (), s32[]{:S(2)}) async-start(), calls=%async_computation.12 | async-start | bytes 5013504 | tf_op jit(solution)/shard_map/all_gather | solution.py:135
  9.4 43.6 %collective-permute-start = (bf16[192,768]{1,0:T(8,128)(2,1)}, bf16[192,768]{1,0:T(8,128)(2,1)S(1)}, u32[]{:S(2)}, u32[]{:S(2)}) collective-permute-start(bf16[192,768]{1,0:T(8,128)(2,1)} %param.26), channel_id=1, source_target_pairs={{0,2},{2,4},{4,6},{6,8},{8,10},{10,12},{12,14},{14,16},{16,18},{18... | collective-permute-start | bytes 884744 | tf_op jit(solution)/shard_map/ppermute | solution.py:21
  10.0 43.4 %collective-permute-start.1 = (bf16[192,768]{1,0:T(8,128)(2,1)}, bf16[192,768]{1,0:T(8,128)(2,1)S(1)}, u32[]{:S(2)}, u32[]{:S(2)}) collective-permute-start(bf16[192,768]{1,0:T(8,128)(2,1)} %param.26), channel_id=1, source_target_pairs={{0,30},{2,0},{4,2},{6,4},{8,6},{10,8},{12,10},{14,12},{16,14},{18,... | collective-permute-start | bytes 884744 | tf_op jit(solution)/shard_map/ppermute | solution.py:26
  15.0 34.0 %all-to-all-start = ((bf16[2,128,768]{2,1,0:T(8,128)(2,1)}), bf16[2,128,768]{2,1,0:T(8,128)(2,1)S(1)}, u32[]{:S(2)}, u32[]{:S(2)}) async-start(bf16[2,128,768]{2,1,0:T(8,128)(2,1)} %param.14), calls=%async_computation | async-start | bytes 786432 | tf_op jit(solution)/shard_map/all_to_all | solution.py:112
  43.9 4.4 copy-start.14
  49.0 15.9 %all-to-all-start.1 = ((f32[16,1,4608]{2,1,0:T(1,128)}), f32[16,1,4608]{2,1,0:T(1,128)S(1)}, u32[]{:S(2)}, u32[]{:S(2)}) async-start(f32[16,1,4608]{2,1,0:T(1,128)} %copy.61), calls=%async_computation.1 | async-start | bytes 589824 | tf_op jit(solution)/shard_map/all_to_all | solution.py:122
  53.0 15.7 %collective-permute-start.2 = (bf16[192,768]{1,0:T(8,128)(2,1)S(1)}, bf16[192,768]{1,0:T(8,128)(2,1)S(1)}, u32[]{:S(2)}, u32[]{:S(2)}) collective-permute-start(bf16[192,768]{1,0:T(8,128)(2,1)S(1)} %collective-permute-done), channel_id=1, source_target_pairs={{0,2},{2,4},{4,6},{6,8},{8,10},{10,12},{12,14},{14,16},{16,18},{18... | collective-permute-start | bytes 884744 | tf_op jit(solution)/shard_map/ppermute | solution.py:21
  53.3 15.5 %collective-permute-start.3 = (bf16[192,768]{1,0:T(8,128)(2,1)S(1)}, bf16[192,768]{1,0:T(8,128)(2,1)S(1)}, u32[]{:S(2)}, u32[]{:S(2)}) collective-permute-start(bf16[192,768]{1,0:T(8,128)(2,1)S(1)} %collective-permute-done.1), channel_id=1, source_target_pairs={{0,30},{2,0},{4,2},{6,4},{8,6},{10,8},{12,10},{14,12},{16,14},{18,... | collective-permute-start | bytes 884744 | tf_op jit(solution)/shard_map/ppermute | solution.py:26
  64.9 14.3 %all-to-all-start.3 = ((bf16[2,128,768]{2,1,0:T(8,128)(2,1)}), bf16[2,128,768]{2,1,0:T(8,128)(2,1)S(1)}, u32[]{:S(2)}, u32[]{:S(2)}) async-start(bf16[2,128,768]{2,1,0:T(8,128)(2,1)} %param.16), calls=%async_computation.3 | async-start | bytes 786432 | tf_op jit(solution)/shard_map/all_to_all | solution.py:113
  68.4 233.4 %reduce-scatter.7.cloned.1.call-start = ((), (), s32[]{:S(2)}) async-start(), calls=%async_computation.14 | async-start | bytes 1216512 | tf_op jit(solution)/shard_map/reduce_scatter | solution.py:63
  68.7 10.5 %collective-permute-start.4 = (bf16[192,768]{1,0:T(8,128)(2,1)S(1)}, bf16[192,768]{1,0:T(8,128)(2,1)S(1)}, u32[]{:S(2)}, u32[]{:S(2)}) collective-permute-start(bf16[192,768]{1,0:T(8,128)(2,1)S(1)} %collective-permute-done.2), channel_id=1, source_target_pairs={{0,2},{2,4},{4,6},{6,8},{8,10},{10,12},{12,14},{14,16},{16,18},{18... | collective-permute-start | bytes 884744 | tf_op jit(solution)/shard_map/ppermute | solution.py:21
  68.8 11.2 %collective-permute-start.5 = (bf16[192,768]{1,0:T(8,128)(2,1)S(1)}, bf16[192,768]{1,0:T(8,128)(2,1)S(1)}, u32[]{:S(2)}, u32[]{:S(2)}) collective-permute-start(bf16[192,768]{1,0:T(8,128)(2,1)S(1)} %collective-permute-done.3), channel_id=1, source_target_pairs={{0,30},{2,0},{4,2},{6,4},{8,6},{10,8},{12,10},{14,12},{16,14},{18,... | collective-permute-start | bytes 884744 | tf_op jit(solution)/shard_map/ppermute | solution.py:26
  79.2 9.3 %collective-permute-start.6 = (bf16[192,768]{1,0:T(8,128)(2,1)S(1)}, bf16[192,768]{1,0:T(8,128)(2,1)}, u32[]{:S(2)}, u32[]{:S(2)}) collective-permute-start(bf16[192,768]{1,0:T(8,128)(2,1)S(1)} %collective-permute-done.4), channel_id=1, source_target_pairs={{0,2},{2,4},{4,6},{6,8},{8,10},{10,12},{12,14},{14,16},{16,18},{18... | collective-permute-start | bytes 884744 | tf_op jit(solution)/shard_map/ppermute | solution.py:21
  80.1 10.0 %collective-permute-start.7 = (bf16[192,768]{1,0:T(8,128)(2,1)S(1)}, bf16[192,768]{1,0:T(8,128)(2,1)S(1)}, u32[]{:S(2)}, u32[]{:S(2)}) collective-permute-start(bf16[192,768]{1,0:T(8,128)(2,1)S(1)} %collective-permute-done.5), channel_id=1, source_target_pairs={{0,30},{2,0},{4,2},{6,4},{8,6},{10,8},{12,10},{14,12},{16,14},{18,... | collective-permute-start | bytes 884744 | tf_op jit(solution)/shard_map/ppermute | solution.py:26
  88.5 11.3 %collective-permute-start.8 = (bf16[192,768]{1,0:T(8,128)(2,1)}, bf16[192,768]{1,0:T(8,128)(2,1)S(1)}, u32[]{:S(2)}, u32[]{:S(2)}) collective-permute-start(bf16[192,768]{1,0:T(8,128)(2,1)} %collective-permute-done.6), channel_id=1, source_target_pairs={{0,2},{2,4},{4,6},{6,8},{8,10},{10,12},{12,14},{14,16},{16,18},{18... | collective-permute-start | bytes 884744 | tf_op jit(solution)/shard_map/ppermute | solution.py:21
  90.0 12.3 %collective-permute-start.9 = (bf16[192,768]{1,0:T(8,128)(2,1)S(1)}, bf16[192,768]{1,0:T(8,128)(2,1)S(1)}, u32[]{:S(2)}, u32[]{:S(2)}) collective-permute-start(bf16[192,768]{1,0:T(8,128)(2,1)S(1)} %collective-permute-done.7), channel_id=1, source_target_pairs={{0,30},{2,0},{4,2},{6,4},{8,6},{10,8},{12,10},{14,12},{16,14},{18,... | collective-permute-start | bytes 884744 | tf_op jit(solution)/shard_map/ppermute | solution.py:26
  99.8 9.3 %collective-permute-start.10 = (bf16[192,768]{1,0:T(8,128)(2,1)S(1)}, bf16[192,768]{1,0:T(8,128)(2,1)S(1)}, u32[]{:S(2)}, u32[]{:S(2)}) collective-permute-start(bf16[192,768]{1,0:T(8,128)(2,1)S(1)} %collective-permute-done.8), channel_id=1, source_target_pairs={{0,2},{2,4},{4,6},{6,8},{8,10},{10,12},{12,14},{14,16},{16,18},{18... | collective-permute-start | bytes 884744 | tf_op jit(solution)/shard_map/ppermute | solution.py:21
  102.3 8.6 %collective-permute-start.11 = (bf16[192,768]{1,0:T(8,128)(2,1)S(1)}, bf16[192,768]{1,0:T(8,128)(2,1)S(1)}, u32[]{:S(2)}, u32[]{:S(2)}) collective-permute-start(bf16[192,768]{1,0:T(8,128)(2,1)S(1)} %collective-permute-done.9), channel_id=1, source_target_pairs={{0,30},{2,0},{4,2},{6,4},{8,6},{10,8},{12,10},{14,12},{16,14},{18,... | collective-permute-start | bytes 884744 | tf_op jit(solution)/shard_map/ppermute | solution.py:26
  109.1 8.9 %collective-permute-start.12 = (bf16[192,768]{1,0:T(8,128)(2,1)S(1)}, bf16[192,768]{1,0:T(8,128)(2,1)S(1)}, u32[]{:S(2)}, u32[]{:S(2)}) collective-permute-start(bf16[192,768]{1,0:T(8,128)(2,1)S(1)} %collective-permute-done.10), channel_id=1, source_target_pairs={{0,2},{2,4},{4,6},{6,8},{8,10},{10,12},{12,14},{14,16},{16,18},{18... | collective-permute-start | bytes 884744 | tf_op jit(solution)/shard_map/ppermute | solution.py:21
  110.9 12.5 %collective-permute-start.13 = (bf16[192,768]{1,0:T(8,128)(2,1)S(1)}, bf16[192,768]{1,0:T(8,128)(2,1)S(1)}, u32[]{:S(2)}, u32[]{:S(2)}) collective-permute-start(bf16[192,768]{1,0:T(8,128)(2,1)S(1)} %collective-permute-done.11), channel_id=1, source_target_pairs={{0,30},{2,0},{4,2},{6,4},{8,6},{10,8},{12,10},{14,12},{16,14},{18,... | collective-permute-start | bytes 884744 | tf_op jit(solution)/shard_map/ppermute | solution.py:26
  118.1 14.4 %collective-permute-start.14 = (bf16[192,768]{1,0:T(8,128)(2,1)S(1)}, bf16[192,768]{1,0:T(8,128)(2,1)S(1)}, u32[]{:S(2)}, u32[]{:S(2)}) collective-permute-start(bf16[192,768]{1,0:T(8,128)(2,1)S(1)} %collective-permute-done.12), channel_id=1, source_target_pairs={{0,2},{2,4},{4,6},{6,8},{8,10},{10,12},{12,14},{14,16},{16,18},{18... | collective-permute-start | bytes 884744 | tf_op jit(solution)/shard_map/ppermute | solution.py:21
  164.7 4.0 copy-start.11
  164.7 10.4 %slice-start = ((s8[4718592]{0:T(1024)(128)(4,1)}), s8[4194304]{0:T(1024)(128)(4,1)S(1)}, s32[]{:S(2)}) async-start(s8[4718592]{0:T(1024)(128)(4,1)} %bitcast.187), calls=%async_computation.18 | async-start | bytes 8388608
  168.7 8.1 %copy-start.16 = (f32[256,3072]{1,0:T(8,128)}, f32[256,3072]{1,0:T(8,128)S(1)}, u32[]{:S(2)}) copy-start(f32[256,3072]{1,0:T(8,128)S(1)} %convolution_add_fusion.1) | copy-start | bytes 9437188
  168.7 6.4 slice-start.1
  175.1 1.7 copy-start.5
  176.8 6.4 copy-start.3
  182.4 0.8 copy-start.8
  184.6 4.8 copy-start.10
  189.5 1.9 copy-start.1
  194.8 2.6 copy-start.7
  194.9 2.5 copy-start.9
  206.1 152.7 %all-gather.13.cloned.1.call-start = ((), (), s32[]{:S(2)}) async-start(), calls=%async_computation.17 | async-start | bytes 1419264 | tf_op jit(solution)/shard_map/all_gather | solution.py:235
  206.1 3.1 copy-start.2
  210.2 256.2 %reduce-scatter.5.cloned.1.call-start = ((), (), s32[]{:S(2)}) async-start(), calls=%async_computation.13 | async-start | bytes 3649536 | tf_op jit(solution)/shard_map/reduce_scatter | solution.py:63
  213.4 1.4 copy-start.6
  213.5 365.0 %reduce-scatter.9.cloned.1.call-start = ((), (), s32[]{:S(2)}) async-start(), calls=%async_computation.15 | async-start | bytes 4866048 | tf_op jit(solution)/shard_map/reduce_scatter | solution.py:63
  218.6 1.0 copy-start.12
  218.6 471.9 %reduce-scatter.11.cloned.1.call-start = ((), (), s32[]{:S(2)}) async-start(), calls=%async_computation.16 | async-start | bytes 4866048 | tf_op jit(solution)/shard_map/reduce_scatter | solution.py:63
  225.9 1.0 copy-start.13
  225.9 9.4 %copy-start.4 = (f32[256,768]{1,0:T(8,128)S(1)}, f32[256,768]{1,0:T(8,128)}, u32[]{:S(2)}) copy-start(f32[256,768]{1,0:T(8,128)} %get-tuple-element.43) | copy-start | bytes 2359300
  231.9 10.7 %all-to-all-start.2 = ((bf16[2,2,49152]{2,1,0:T(2,128)(2,1)}), bf16[2,2,49152]{2,1,0:T(2,128)(2,1)S(1)}, u32[]{:S(2)}, u32[]{:S(2)}) async-start(bf16[2,2,49152]{2,1,0:T(2,128)(2,1)} %reshape.788), calls=%async_computation.2 | async-start | bytes 786432 | tf_op jit(solution)/shard_map/all_to_all | solution.py:169
  242.6 16.3 %all-to-all-start.4 = ((f32[1,256,768]{2,0,1:T(1,128)}), f32[1,256,768]{2,0,1:T(1,128)S(1)}, u32[]{:S(2)}, u32[]{:S(2)}) async-start(f32[1,256,768]{2,0,1:T(1,128)} %copy.70), calls=%async_computation.4 | async-start | bytes 1572864 | tf_op jit(solution)/shard_map/all_to_all | solution.py:221
  303.2 70.2 %copy-start.15 = (bf16[2,768]{1,0:T(2,128)(2,1)S(1)}, bf16[2,768]{1,0:T(2,128)(2,1)}, u32[]{:S(2)}) copy-start(bf16[2,768]{1,0:T(2,128)(2,1)} %param.15) | copy-start | bytes 9220
  361.1 11.0 %all-to-all-start.5 = ((f32[16,1,96]{2,1,0:T(1,128)}), f32[16,1,96]{2,1,0:T(1,128)S(1)}, u32[]{:S(2)}, u32[]{:S(2)}) async-start(f32[16,1,96]{2,1,0:T(1,128)} %bitcast.31), calls=%async_computation.5 | async-start | bytes 16384 | tf_op jit(solution)/shard_map/all_to_all | solution.py:259
Sparse Core Ops, SparseCore 0:
  10.3 55.3 all-gather.6
  68.0 40.5 all-gather.8
  110.9 53.7 all-gather.10
  206.2 95.5 reduce-scatter.6
  305.1 53.6 all-gather.12
  364.1 102.3 reduce-scatter.4
  471.9 106.5 reduce-scatter.8
  584.0 106.4 reduce-scatter.10
